TPU v7x, 32 devices: a whole 2x2x4 slice. The times are simulated.
32 devices in a mesh: seg: 8 (over z, y), col: 4 (over x, core).
Axes of the slice: x: 2, y: 2, z: 4, core: 2. Of those that a mesh axis runs over, the one named last changes fastest.
Arguments:
- left_image: bfloat16 [65536, 2048], P('seg', 'col'), may hold values from -130 to 130
- right_image: bfloat16 [65536, 2048], P('seg', 'col'), may hold values from -130 to 130
- peak_offsets: int32 [2, 128, 4], P(None, 'seg', 'col'), may hold values from -15 to 15
- match_owner: int32 [114688, 1], P(('seg', 'col')), may hold values from 0 to 31; in each aligned block of 3584 rows (0 to 3583, 3584 to 7167, ...) at most 280 rows name the same one
- match_source: int32 [114688], P(('seg', 'col')), may hold values from 0 to 8191
- match_line: int32 [114688], P(('seg', 'col')), may hold values from 0 to 2047
Outputs:
- diag_blocks: float32 [6, 16384], P(None, ('seg', 'col'))
- coupling_blocks: float32 [6, 16384], P(None, ('seg', 'col'))
- normal_rhs: float32 [3, 16384], P(None, ('seg', 'col'))
Inputs may be any that keep to these rules, and one draw needn't show every extreme that they name: `match_owner`: among the rows of one device, no owner is named by more than 280 matches.
All inputs are finite; a program needn't handle non-finite values.
Results may differ from a plain program's by a relative error of at most 0.0003.
Values may be sent and summed in bfloat16 or wider, within the bound.
A program may use at most 128 MiB of HBM per device.

v0:
```python
import jax
import jax.numpy as jnp
from jax import lax
from jax.sharding import PartitionSpec as P

TILE = 512
RANGE = 15
SAMP = 4


EPSILON = 1e-05
SHARPNESS = 6.0
JACOBIAN_A = 0.5
JACOBIAN_B = -0.3
JACOBIAN_C = -0.8


def padded(shard, sides, width):
    for axis, dim in sides:
        size, length = (lax.axis_size(axis), shard.shape[dim])
        up = [(i, (i + 1) % size) for i in range(size - 1)]
        down = [(j, i) for i, j in up]
        last = lax.slice_in_dim(shard, length - width, length, axis=dim)
        first = lax.slice_in_dim(shard, 0, width, axis=dim)
        before = lax.ppermute(last, axis, up)
        after = lax.ppermute(first, axis, down)
        shard = jnp.concatenate([before, shard, after], axis=dim)
    return shard


def shifted(value, axis, steps):
    count = lax.axis_size(axis)
    first, last = (max(0, -steps), min(count, count - steps))
    return lax.ppermute(value, axis, [(source, source + steps) for source in range(first, last)])


def tile_observations(window, left_tile, offset_row, offset_col):
    tile_lines = left_tile.shape[0]
    pixels = left_tile.shape[1]
    pixel_count = float(pixels)
    left_vals = left_tile.astype(jnp.float32)
    left_sum = jnp.sum(left_vals, axis=1)
    left_var = (
        jnp.sum(left_vals * left_vals, axis=1)
        - left_sum * left_sum / pixel_count
        + pixel_count * EPSILON
    )
    table = {}
    for col_step in range(3):
        right_cols = window[:, col_step : col_step + pixels].astype(jnp.float32)
        line_sum = jnp.sum(right_cols, axis=1)
        line_square = jnp.sum(right_cols * right_cols, axis=1)
        for row_step in range(3):
            right_vals = right_cols[row_step : row_step + tile_lines]
            right_sum = line_sum[row_step : row_step + tile_lines]
            right_var = (
                line_square[row_step : row_step + tile_lines]
                - right_sum * right_sum / pixel_count
                + pixel_count * EPSILON
            )
            covariance = (
                jnp.sum(left_vals * right_vals, axis=1) - left_sum * right_sum / pixel_count
            )
            table[row_step, col_step] = covariance / jnp.sqrt(left_var * right_var)
    scores = jnp.stack(
        [table[row_step, col_step] for row_step in range(3) for col_step in range(3)]
    )
    exp_scores = jnp.exp(SHARPNESS * scores)
    denominator = jnp.sum(exp_scores, axis=0)
    shift_row = (jnp.sum(exp_scores[6:], axis=0) - jnp.sum(exp_scores[:3], axis=0)) / denominator
    shift_col = (
        jnp.sum(exp_scores[2::3], axis=0) - jnp.sum(exp_scores[0::3], axis=0)
    ) / denominator
    offset_scale = 1.0 / (RANGE + 1)
    resid_row = (offset_row.astype(jnp.float32) + shift_row) * offset_scale
    resid_col = (offset_col.astype(jnp.float32) + shift_col) * offset_scale
    weight = 0.2 * (0.1 + scores[4] * scores[4])
    return jnp.stack([resid_row, resid_col, weight])


def normal_terms(resid_row, resid_col, weight, spread):
    unity = jnp.ones_like(spread)
    along_track = [JACOBIAN_A * spread, unity, spread]
    across = [unity, JACOBIAN_B * spread, JACOBIAN_C * spread]
    index_pairs = ((0, 0), (0, 1), (0, 2), (1, 1), (1, 2), (2, 2))
    moment = jnp.stack(
        [
            weight
            * (
                along_track[first_index] * along_track[second_index]
                + across[first_index] * across[second_index]
            )
            for first_index, second_index in index_pairs
        ],
        axis=0,
    )
    gradient = jnp.stack(
        [
            weight * (along_track[first_index] * resid_row + across[first_index] * resid_col)
            for first_index in range(3)
        ],
        axis=0,
    )
    return (moment, gradient)


def line_fraction(line_ids):
    return ((line_ids % SAMP).astype(jnp.float32) + 0.5) / SAMP


def bin_terms(moment, gradient, sample_ids, fraction, bin_count):
    near_weight = 1.0 - fraction
    next_ids = sample_ids + 1
    diagonal = (
        jnp.zeros((6, bin_count), jnp.float32)
        .at[:, sample_ids]
        .add(moment * (near_weight * near_weight)[None, :], mode="drop")
    )
    diagonal = diagonal.at[:, next_ids].add(moment * (fraction * fraction)[None, :], mode="drop")
    coupling = (
        jnp.zeros((6, bin_count), jnp.float32)
        .at[:, sample_ids]
        .add(moment * (fraction * near_weight)[None, :], mode="drop")
    )
    right_side = (
        jnp.zeros((3, bin_count), jnp.float32)
        .at[:, sample_ids]
        .add(gradient * near_weight[None, :], mode="drop")
    )
    right_side = right_side.at[:, next_ids].add(gradient * fraction[None, :], mode="drop")
    return (diagonal, coupling, right_side)


def local(left_image, right_image, peak_offsets, match_owner, match_source, match_line):
    rim_width = RANGE + 1
    rows_dev = left_image.shape[0]
    seg_count = lax.axis_size("seg")
    col_count = lax.axis_size("col")
    device_count = seg_count * col_count
    samp_own = rows_dev // (SAMP * col_count)
    extended = padded(right_image, (("seg", 0), ("col", 1)), rim_width)

    def one_tile(tile_index):
        offset_row = peak_offsets[0, tile_index, 0]
        offset_col = peak_offsets[1, tile_index, 0]
        window = lax.dynamic_slice(
            extended,
            (tile_index * TILE + rim_width + offset_row - 1, rim_width + offset_col - 1),
            (TILE + 2, TILE + 2),
        )
        left_tile = lax.dynamic_slice_in_dim(left_image, tile_index * TILE, TILE, 0)
        return tile_observations(window, left_tile, offset_row, offset_col)

    observations = lax.map(one_tile, jnp.arange(rows_dev // TILE, dtype=jnp.int32))
    records = observations[match_source // TILE, :, match_source % TILE]
    column = lax.axis_index("col")
    spread = jnp.full(
        match_source.shape, 2.0 * (column.astype(jnp.float32) + 0.5) / col_count - 1.0, jnp.float32
    )
    owner_ids = match_owner[:, 0]
    capacity = 5 * match_source.shape[0] // (2 * device_count)
    member = (owner_ids[:, None] == jnp.arange(device_count, dtype=jnp.int32)[None, :]).astype(
        jnp.int32
    )
    slot_ids = jnp.sum((jnp.cumsum(member, axis=0) - 1) * member, axis=1)
    position = owner_ids * capacity + slot_ids
    fields = jnp.stack([records[:, 0], records[:, 1], records[:, 2], spread])
    outgoing = jnp.zeros((4, device_count * capacity), jnp.float32).at[:, position].set(fields)
    line_ids = (
        jnp.zeros((1, device_count * capacity), jnp.int32).at[:, position].set(match_line[None, :])
    )
    received, received_lines = (
        lax.all_to_all(
            outgoing.reshape(4, device_count, capacity),
            ("seg", "col"),
            split_axis=1,
            concat_axis=1,
            tiled=True,
        ),
        lax.all_to_all(
            line_ids.reshape(1, device_count, capacity),
            ("seg", "col"),
            split_axis=1,
            concat_axis=1,
            tiled=True,
        ),
    )
    fields_in = received.reshape(4, -1)
    lines_in = received_lines.reshape(-1)
    moment, gradient = normal_terms(fields_in[0], fields_in[1], fields_in[2], fields_in[3])
    diagonal, coupling, right_side = bin_terms(
        moment, gradient, lines_in // SAMP, line_fraction(lines_in), samp_own + 1
    )
    carried_diag, carried_rhs = shifted(
        (diagonal[:, samp_own:], right_side[:, samp_own:]), ("seg", "col"), 1
    )
    diag_blocks = diagonal[:, :samp_own].at[:, 0:1].add(carried_diag)
    normal_rhs = right_side[:, :samp_own].at[:, 0:1].add(carried_rhs)
    coupling_blocks = coupling[:, :samp_own]
    return (diag_blocks, coupling_blocks, normal_rhs)


def solution(mesh):
    return jax.shard_map(
        local,
        mesh=mesh,
        in_specs=(
            P("seg", "col"),
            P("seg", "col"),
            P(None, "seg", "col"),
            P(("seg", "col"), None),
            P(("seg", "col")),
            P(("seg", "col")),
        ),
        out_specs=(P(None, ("seg", "col")), P(None, ("seg", "col")), P(None, ("seg", "col"))),
        check_vma=False,
    )
```

profile of v0, /device:TPU:0, one launch (start us, length us, event | category | flops | bytes accessed | tf_op | source)
XLA Modules:
  0.0 809.4 jit_solution(4686471080137359560)
XLA Ops:
  1.5 4.9 collective-permute-start
  8.6 9.2 %reduce-window.6 = s32[32,28,128]{2,1,0:T(8,128)S(1)} reduce-window(s32[32,28,128]{2,1,0:T(8,128)S(1)} %fusion.14, s32[]{:T(128)} %constant.313.clone.1), window={size=1x1x128 pad=0_0x0_0x127_0}, to_apply=%region_0.1 | reduce-window | flops 14565376 | bytes 917508 | tf_op jit(solution)/shard_map/reduce-window
  19.4 11.4 %copy.49 = bf16[8192,512]{0,1:T(8,128)(2,1)} copy(bf16[8192,512]{1,0:T(8,128)(2,1)} %param.13) | data formatting | bytes 16777216 | tf_op args[1]
  30.8 18.0 %concatenate.13 = bf16[8224,512]{0,1:T(8,128)(2,1)} concatenate(bf16[16,512]{0,1:T(8,128)(2,1)S(1)} %collective-permute-done, bf16[8192,512]{0,1:T(8,128)(2,1)} %copy.49, bf16[16,512]{0,1:T(8,128)(2,1)S(1)} %collective-permute-done.1), dimensions={0} | concatenate | bytes 16842752 | tf_op jit(solution)/shard_map/concatenate | solution.py:27
  52.8 13.8 %scatter_custom_fusion = s32[8960]{0:T(1024)S(1)} fusion(s32[3584]{0:T(1024)S(1)} %fusion.40, s32[3584]{0:T(1024)} %param.17, s32[]{:T(128)} %constant.313.clone.1), kind=kCustom, calls=%fused_computation.122 | custom fusion | bytes 36352 | tf_op jit(solution)/shard_map/scatter | solution.py:170
  67.4 9.9 %all-to-all-start = ((s32[1,32,280]{2,0,1:T(1,128)}), s32[1,32,280]{2,0,1:T(1,128)S(1)}, u32[]{:S(2)}, u32[]{:S(2)}) async-start(s32[1,32,280]{2,0,1:T(1,128)} %reshape.638), calls=%async_computation | async-start | bytes 98304 | tf_op jit(solution)/shard_map/all_to_all | solution.py:180
  78.8 5.7 all-to-all-done
  84.8 9.3 %pad_maximum_fusion = bf16[8224,544]{0,1:T(8,128)(2,1)} fusion(bf16[8224,16]{0,1:T(8,128)(2,1)S(1)} %collective-permute-done.3, bf16[8224,512]{0,1:T(8,128)(2,1)} %concatenate.13, bf16[8224,16]{0,1:T(8,128)(2,1)S(1)} %collective-permute-done.2), kind=kLoop, calls=%fused_computation.59 | loop fusion | flops 26843136 | bytes 17895424 | tf_op jit(solution)/shard_map/concatenate | solution.py:27
  94.6 327.2 %while.17 = (s32[]{:T(128)}, f32[16,3,512]{2,1,0:T(4,128)S(1)}, s32[16]{0:T(128)}, s32[2,16,1]{1,2,0:T(1,128)S(1)}, bf16[8192,512]{1,0:T(8,128)(2,1)}, /*index=5...) while((s32[]{:T(128)}, f32[16,3,512]{2,1,0:T(4,128)S(1)}, ...), condition=%wide.region_27.28_spmd, body=%wide.region_4.27_spmd.sunk | while | flops 9775115 | bytes 33405588 | solution.py:154
  121.0 4.0 fusion.50
  141.5 4.0 fusion.50
  284.5 4.1 fusion.50
  366.3 4.0 fusion.50
  386.7 4.1 fusion.50
  424.4 35.5 %gather_fusion = f32[3584,3]{1,0:T(8,128)S(1)} fusion(f32[16,3,512]{1,2,0:T(8,128)} %copy.51, s32[3584]{0:T(1024)S(1)} %fusion.33), kind=kCustom, calls=%fused_computation | custom fusion | bytes 114688 | tf_op jit(solution)/shard_map/gather | solution.py:155
  463.2 11.8 %scatter_custom_fusion.1 = f32[4,8960]{0,1:T(8,128)} fusion(s32[3584]{0:T(1024)} %copy-done.7, f32[3584,4]{1,0:T(8,128)S(1)} %copy.52, f32[]{:T(128)} %constant.312.clone.1), kind=kCustom, calls=%fused_computation.60 | custom fusion | bytes 143872 | tf_op jit(solution)/shard_map/scatter | solution.py:168
  475.0 4.1 copy.53
  482.4 8.2 %all-to-all-done.1 = f32[4,32,280]{2,0,1:T(4,128)S(1)} async-done(((f32[4,32,280]{2,0,1:T(4,128)}), f32[4,32,280]{2,0,1:T(4,128)S(1)}, u32[]{:S(2)}, u32[]{:S(2)}) %all-to-all-start.1) | async-done | bytes 143392 | tf_op jit(solution)/shard_map/all_to_all | solution.py:173
  497.8 58.1 %scatter_custom_fusion.5 = f32[3,513]{0,1:T(8,128)S(1)} fusion(s32[8960]{0:T(1024)S(1)} %get-tuple-element.235, f32[8960,3]{1,0:T(8,128)} %copy.57, f32[]{:T(128)} %constant.312.clone.1), kind=kCustom, calls=%fused_computation.82 | custom fusion | flops 26880 | bytes 6668 | tf_op jit(solution)/shard_map/scatter-add | solution.py:128
  555.9 58.1 %scatter_fusion.1 = f32[3,513]{0,1:T(8,128)S(1)} fusion(f32[3,513]{0,1:T(8,128)S(1)} %scatter_custom_fusion.5, s32[8960]{0:T(1024)S(1)} %get-tuple-element.234, f32[8960,3]{1,0:T(8,128)} %copy.58), kind=kCustom, calls=%fused_computation.7 | custom fusion | flops 26880 | bytes 358400 | tf_op jit(solution)/shard_map/scatter-add | solution.py:130
  617.3 58.1 %scatter_custom_fusion.2 = f32[6,513]{0,1:T(8,128)S(1)} fusion(s32[8960]{0:T(1024)S(1)} %get-tuple-element.235, f32[8960,6]{1,0:T(8,128)} %copy.54, f32[]{:T(128)} %constant.312.clone.1), kind=kCustom, calls=%fused_computation.86 | custom fusion | flops 53760 | bytes 12824 | tf_op jit(solution)/shard_map/scatter-add | solution.py:117
  678.3 58.3 %scatter_fusion = f32[6,513]{0,1:T(8,128)S(1)} fusion(f32[6,513]{0,1:T(8,128)S(1)} %scatter_custom_fusion.2, s32[8960]{0:T(1024)S(1)} %get-tuple-element.234, f32[8960,6]{1,0:T(8,128)} %copy.55), kind=kCustom, calls=%fused_computation.4 | custom fusion | flops 53760 | bytes 680960 | tf_op jit(solution)/shard_map/scatter-add | solution.py:119
  736.7 6.3 collective-permute-start.5
  747.7 58.1 %scatter_custom_fusion.4 = f32[6,513]{0,1:T(8,128)S(1)} fusion(s32[8960]{0:T(1024)S(1)} %get-tuple-element.235, f32[8960,6]{1,0:T(8,128)} %copy.56, f32[]{:T(128)} %constant.312.clone.1), kind=kCustom, calls=%fused_computation.84 | custom fusion | flops 53760 | bytes 12824 | tf_op jit(solution)/shard_map/scatter-add | solution.py:123
  (631 shorter events, 262.8 us)
Async XLA Ops:
  1.5 29.3 %collective-permute-start = (bf16[16,512]{0,1:T(8,128)(2,1)S(1)}, bf16[16,512]{0,1:T(8,128)(2,1)S(1)}, u32[]{:S(2)}, u32[]{:S(2)}) collective-permute-start(bf16[16,512]{0,1:T(8,128)(2,1)S(1)} %copy.47), channel_id=1, source_target_pairs={{0,4},{4,8},{8,12},{12,16},{16,20},{20,24},{24,28},{1,5},{5,9},{9,... | collective-permute-start | bytes 49160 | tf_op jit(solution)/shard_map/ppermute | solution.py:25
  6.5 24.3 %collective-permute-start.1 = (bf16[16,512]{0,1:T(8,128)(2,1)S(1)}, bf16[16,512]{0,1:T(8,128)(2,1)S(1)}, u32[]{:S(2)}, u32[]{:S(2)}) collective-permute-start(bf16[16,512]{0,1:T(8,128)(2,1)S(1)} %copy.48), channel_id=1, source_target_pairs={{4,0},{8,4},{12,8},{16,12},{20,16},{24,20},{28,24},{5,1},{9,5},{13... | collective-permute-start | bytes 49160 | tf_op jit(solution)/shard_map/ppermute | solution.py:26
  30.8 21.9 %copy-start.5 = (s32[3584,1]{0,1:T(1,128)S(1)}, s32[3584,1]{0,1:T(1,128)}, u32[]{:S(2)}) copy-start(s32[3584,1]{0,1:T(1,128)} %param.15) | copy-start | bytes 43012
  30.8 46.6 %copy-start.8 = (s32[3584]{0:T(1024)S(1)}, s32[3584]{0:T(1024)}, u32[]{:S(2)}) copy-start(s32[3584]{0:T(1024)} %param.16) | copy-start | bytes 43012
  49.9 34.8 %collective-permute-start.2 = (bf16[8224,16]{0,1:T(8,128)(2,1)S(1)}, bf16[8224,16]{0,1:T(8,128)(2,1)S(1)}, u32[]{:S(2)}, u32[]{:S(2)}) collective-permute-start(bf16[8224,16]{0,1:T(8,128)(2,1)S(1)} %get-tuple-element.267), channel_id=1, source_target_pairs={{0,1},{1,2},{2,3},{4,5},{5,6},{6,7},{8,9},{9,10},{10,11},{12,13},{... | collective-permute-start | bytes 789512 | tf_op jit(solution)/shard_map/ppermute | solution.py:25
  51.4 33.3 %collective-permute-start.3 = (bf16[8224,16]{0,1:T(8,128)(2,1)S(1)}, bf16[8224,16]{0,1:T(8,128)(2,1)S(1)}, u32[]{:S(2)}, u32[]{:S(2)}) collective-permute-start(bf16[8224,16]{0,1:T(8,128)(2,1)S(1)} %get-tuple-element.268), channel_id=1, source_target_pairs={{1,0},{2,1},{3,2},{5,4},{6,5},{7,6},{9,8},{10,9},{11,10},{13,12},{... | collective-permute-start | bytes 789512 | tf_op jit(solution)/shard_map/ppermute | solution.py:26
  52.8 14.6 %copy-start.7 = (s32[3584]{0:T(1024)}, s32[3584]{0:T(1024)S(1)}, u32[]{:S(2)}) copy-start(s32[3584]{0:T(1024)S(1)} %fusion.40) | copy-start | bytes 43012
  67.4 17.1 %all-to-all-start = ((s32[1,32,280]{2,0,1:T(1,128)}), s32[1,32,280]{2,0,1:T(1,128)S(1)}, u32[]{:S(2)}, u32[]{:S(2)}) async-start(s32[1,32,280]{2,0,1:T(1,128)} %reshape.638), calls=%async_computation | async-start | bytes 98304 | tf_op jit(solution)/shard_map/all_to_all | solution.py:180
  84.7 9.9 %copy-start.6 = (s32[2,16,1]{1,2,0:T(1,128)S(1)}, s32[2,16,1]{1,2,0:T(1,128)}, u32[]{:S(2)}) copy-start(s32[2,16,1]{1,2,0:T(1,128)} %param.14) | copy-start | bytes 388
  151.0 3.4 copy-start.1
  171.3 3.4 copy-start.1
  212.2 3.4 copy-start.1
  252.9 3.4 copy-start.1
  273.4 3.4 copy-start.1
  294.0 3.4 copy-start.1
  314.4 3.4 copy-start.1
  334.8 3.4 copy-start.1
  355.2 3.4 copy-start.1
  375.6 3.4 copy-start.1
  396.3 3.4 copy-start.1
  416.6 3.4 copy-start.1
  479.1 11.5 %all-to-all-start.1 = ((f32[4,32,280]{2,0,1:T(4,128)}), f32[4,32,280]{2,0,1:T(4,128)S(1)}, u32[]{:S(2)}, u32[]{:S(2)}) async-start(f32[4,32,280]{2,0,1:T(4,128)} %copy.53), calls=%async_computation.1 | async-start | bytes 393216 | tf_op jit(solution)/shard_map/all_to_all | solution.py:173
  736.7 69.9 %collective-permute-start.5 = (f32[3,1]{0,1:T(1,128)S(1)}, f32[3,1]{0,1:T(1,128)S(1)}, u32[]{:S(2)}, u32[]{:S(2)}) collective-permute-start(f32[3,1]{0,1:T(1,128)S(1)} %slice.488), channel_id=1, source_target_pairs={{0,1},{1,2},{2,3},{3,4},{4,5},{5,6},{6,7},{7,8},{8,9},{9,10},{10,1... | collective-permute-start | bytes 44 | tf_op jit(solution)/shard_map/ppermute | solution.py:34
  743.0 65.0 %collective-permute-start.4 = (f32[6,1]{0,1:T(1,128)S(1)}, f32[6,1]{0,1:T(1,128)S(1)}, u32[]{:S(2)}, u32[]{:S(2)}) collective-permute-start(f32[6,1]{0,1:T(1,128)S(1)} %slice.482), channel_id=1, source_target_pairs={{0,1},{1,2},{2,3},{3,4},{4,5},{5,6},{6,7},{7,8},{8,9},{9,10},{10,1... | collective-permute-start | bytes 80 | tf_op jit(solution)/shard_map/ppermute | solution.py:34
  (69 other events, 133.5 us)
where the time goes:
time: 819 us; the launch traced here: 809 us
  other arithmetic  397 us (48%)
  local copies, waits for them, and re-layouts  281 us (34%)
  loops' own time  86.2 us (11%)
  starting transfers between devices  29.9 us (4%)
  waiting for transfers between devices  13.9 us (2%)
    another operation x1, loops' own time, local(): lax.map(one_tile, jnp.arange(rows_dev // TILE, dtype=jnp.int32))  86.2 us
    while x208, local copies, waits for them, and re-layouts  63.3 us
    slice x16, local copies, waits for them, and re-layouts, tile_observations(): right_cols = window[:, col_step:col_step + pixels].astype(jnp.float32)  62.7 us
    scatter-add x1, other arithmetic, bin_terms(): diagonal.at[:, next_ids]  58.3 us
    scatter-add x1, other arithmetic, bin_terms(): right_side = jnp.zeros((3, bin_count), jnp.float32).at[:, sample_ids].add...  58.1 us
    scatter-add x1, other arithmetic, bin_terms(): diagonal = jnp.zeros((6, bin_count), jnp.float32).at[:, sample_ids].add(m...  58.1 us
    scatter-add x1, other arithmetic, bin_terms(): coupling = jnp.zeros((6, bin_count), jnp.float32).at[:, sample_ids].add(m...  58.1 us
    scatter-add x1, other arithmetic, bin_terms(): right_side.at[:, next_ids].add(gradient * fraction[None, :], mode='drop')  58.1 us
  transfers between devices with their start and end apart: 8, of which 2 were waited for; matrix products, arithmetic and copies ran while one was open for 13% of the time, Pallas kernels for 0%

commit v1 on v0

v1 whole, which is shorter than its diff:
```python
import functools

import jax
import jax.numpy as jnp
from jax import lax
from jax.experimental import pallas as pl
from jax.experimental.pallas import tpu as pltpu
from jax.sharding import PartitionSpec as P

TILE = 512
RANGE = 15
SAMP = 4
RIM = RANGE + 1
LANES = 128
WINDOW = TILE + 2 * RIM
PADDED = TILE + LANES

EPSILON = 1e-05
SHARPNESS = 6.0
JACOBIAN_A = 0.5
JACOBIAN_B = -0.3
JACOBIAN_C = -0.8

F32 = jnp.float32
BF16 = jnp.bfloat16


def iota(shape, dim):
    return lax.broadcasted_iota(jnp.int32, shape, dim)


def rim_rows(tile, tiles, prev_ref, next_ref, above_ref, below_ref):
    before = jnp.where(tile == 0, above_ref[...].astype(F32), prev_ref[...].astype(F32))
    after = jnp.where(tile == tiles - 1, below_ref[...].astype(F32), next_ref[...].astype(F32))
    return before, after


def edge_kernel(tiles, *refs):
    sides, outs = (refs[:5], refs[5:10]), refs[10:]
    tile = pl.program_id(0)
    for side in range(2):
        main_ref, prev_ref, next_ref, above_ref, below_ref = sides[side]
        before, after = rim_rows(tile, tiles, prev_ref, next_ref, above_ref, below_ref)
        wrap = jnp.concatenate(
            [after, jnp.zeros((LANES - 2 * RIM, LANES), F32), before], axis=0
        ).astype(BF16)
        first = 0 if side == 0 else LANES - RIM
        pick = (iota((RIM, LANES), 1) == iota((RIM, LANES), 0) + first).astype(F32).astype(BF16)
        contract = (((1,), (1,)), ((), ()))
        main = lax.dot_general(pick, main_ref[...], contract, preferred_element_type=F32)
        rest = lax.dot_general(pick, wrap, contract, preferred_element_type=F32)
        outs[side][0, :, :TILE] = main.astype(BF16)
        outs[side][0, :, TILE:] = rest.astype(BF16)


def edges(right, above, below):
    lines, pixels = right.shape
    tiles, blocks, per = lines // TILE, lines // RIM, TILE // RIM
    specs, operands = [], []
    for block in (0, pixels // LANES - 1):
        specs += [
            pl.BlockSpec((TILE, LANES), lambda t, block=block: (t, block)),
            pl.BlockSpec((RIM, LANES), lambda t, block=block: (jnp.maximum(t * per - 1, 0), block)),
            pl.BlockSpec(
                (RIM, LANES),
                lambda t, block=block: (jnp.minimum((t + 1) * per, blocks - 1), block),
            ),
            pl.BlockSpec((RIM, LANES), lambda t, block=block: (0, block)),
            pl.BlockSpec((RIM, LANES), lambda t, block=block: (0, block)),
        ]
        operands += [right, right, right, above, below]
    out = jax.ShapeDtypeStruct((tiles, RIM, PADDED), BF16)
    return pl.pallas_call(
        functools.partial(edge_kernel, tiles),
        grid=(tiles,),
        in_specs=specs,
        out_specs=[pl.BlockSpec((1, RIM, PADDED), lambda t: (t, 0, 0))] * 2,
        out_shape=[out, out],
        name="edges",
    )(*operands)


def pick_lines(load, count):
    lane = iota((8, LANES), 1)
    group = lane // 8
    acc = load(0)
    for i in range(1, count):
        acc = jnp.where(group == i, load(i), acc)
    acc = jnp.where(lane % 8 == iota((8, LANES), 0), acc, 0.0)
    return jnp.sum(acc, axis=0, keepdims=True)


def correlate_kernel(
    tiles,
    offsets_ref,
    left_ref,
    main_ref,
    prev_ref,
    next_ref,
    above_ref,
    below_ref,
    west_ref,
    east_ref,
    out_ref,
    shifted_ref,
    halo_ref,
    stat_ref,
    flat_ref,
    gram_ref,
    dots_ref,
    sums_ref,
    squares_ref,
):
    tile = pl.program_id(0)
    offset_row = offsets_ref[0, tile]
    offset_col = offsets_ref[1, tile]
    blocks = TILE // LANES

    contract = (((0,), (0,)), ((), ()))
    spot = iota((RIM, LANES), 1) - iota((RIM, LANES), 0)
    east = lax.dot_general(
        east_ref[0], (spot == 0).astype(F32).astype(BF16), contract, preferred_element_type=F32
    )
    west = lax.dot_general(
        west_ref[0],
        (spot == LANES - RIM).astype(F32).astype(BF16),
        contract,
        preferred_element_type=F32,
    )
    halo_ref[...] = east + west

    def process(values, halo, target):
        rows = values.shape[0]
        parts = [values[:, LANES * b : LANES * (b + 1)] for b in range(blocks)] + [halo]
        lane = iota((rows, LANES), 1)
        for s in range(3):
            step = offset_col + (s - 1)
            turn = lax.rem(LANES - step, LANES)
            turned = [pltpu.roll(part, turn, 1) for part in parts]
            source = lane + step
            low, high = source < 0, source >= LANES
            total = squares = None
            for b in range(blocks):
                value = jnp.where(
                    low, turned[b - 1], jnp.where(high, turned[b + 1], turned[b])
                )
                total = value if b == 0 else total + value
                squares = value * value if b == 0 else squares + value * value
                shifted_ref[s, pl.ds(target, rows), LANES * b : LANES * (b + 1)] = value.astype(BF16)
            stat_ref[s, pl.ds(target, rows), :] = jnp.broadcast_to(
                jnp.sum(total, axis=1, keepdims=True), (rows, LANES)
            )
            stat_ref[3 + s, pl.ds(target, rows), :] = jnp.broadcast_to(
                jnp.sum(squares, axis=1, keepdims=True), (rows, LANES)
            )

    before, after = rim_rows(tile, tiles, prev_ref, next_ref, above_ref, below_ref)
    process(before, halo_ref[PADDED - RIM :, :], 0)
    process(after, halo_ref[TILE : TILE + RIM, :], RIM + TILE)
    chunk = 32

    @pl.loop(0, TILE // chunk)
    def _(index):
        start = pl.multiple_of(index * chunk, chunk)
        process(
            main_ref[pl.ds(start, chunk), :].astype(F32),
            halo_ref[pl.ds(start, chunk), :],
            pl.multiple_of(start + RIM, RIM),
        )
        left = left_ref[pl.ds(start, chunk), :].astype(F32)
        parts = [left[:, LANES * b : LANES * (b + 1)] for b in range(blocks)]
        total = parts[0] + parts[1] + parts[2] + parts[3]
        squares = sum(part * part for part in parts[1:]) + parts[0] * parts[0]
        stat_ref[6, pl.ds(start, chunk), :] = jnp.broadcast_to(
            jnp.sum(total, axis=1, keepdims=True), (chunk, LANES)
        )
        stat_ref[7, pl.ds(start, chunk), :] = jnp.broadcast_to(
            jnp.sum(squares, axis=1, keepdims=True), (chunk, LANES)
        )

    for k in range(8):
        for b in range(5 if k < 6 else 4):
            flat_ref[k : k + 1, LANES * b : LANES * (b + 1)] = pick_lines(
                lambda i: stat_ref[k, LANES * b + 8 * i : LANES * b + 8 * i + 8, :],
                16 if b < 4 else 4,
            )

    lane = iota((8, LANES), 1)
    for r in range(3):
        start = offset_row + (RANGE + r)
        turn = lax.rem(LANES - start, LANES)
        turned = [
            pltpu.roll(flat_ref[:, LANES * b : LANES * (b + 1)], turn, 1) for b in range(blocks + 1)
        ]
        for b in range(blocks):
            value = jnp.where(lane < LANES - start, turned[b], turned[b + 1])
            sums_ref[3 * r : 3 * r + 3, LANES * b : LANES * (b + 1)] = value[0:3]
            squares_ref[3 * r : 3 * r + 3, LANES * b : LANES * (b + 1)] = value[3:6]

    for b in range(blocks):
        for s in range(3):
            gram_ref[b, s] = lax.dot_general(
                shifted_ref[s, LANES * b : LANES * b + LANES + 2 * RIM, :],
                left_ref[LANES * b : LANES * (b + 1), :],
                (((1,), (1,)), ((), ())),
                preferred_element_type=F32,
            )
        for r in range(3):
            start = offset_row + (RANGE + r)
            for s in range(3):
                dots_ref[3 * r + s : 3 * r + s + 1, LANES * b : LANES * (b + 1)] = pick_lines(
                    lambda i: gram_ref[b, s, pl.ds(start + 8 * i, 8), :], 16
                )

    count = float(TILE)
    left_sum = flat_ref[6:7, :TILE]
    left_var = flat_ref[7:8, :TILE] - left_sum * left_sum / count + count * EPSILON
    right_sum = sums_ref[0:9, :]
    right_var = squares_ref[0:9, :] - right_sum * right_sum / count + count * EPSILON
    covariance = dots_ref[0:9, :] - left_sum * right_sum / count
    scores = covariance / jnp.sqrt(left_var * right_var)
    weights = jnp.exp(SHARPNESS * scores)
    row = [weights[i : i + 1] for i in range(9)]
    denominator = sum(row[1:], row[0])
    shift_row = ((row[6] + row[7] + row[8]) - (row[0] + row[1] + row[2])) / denominator
    shift_col = ((row[2] + row[5] + row[8]) - (row[0] + row[3] + row[6])) / denominator
    scale = 1.0 / (RANGE + 1)
    out_ref[0, 0:1, :] = (offset_row.astype(F32) + shift_row) * scale
    out_ref[0, 1:2, :] = (offset_col.astype(F32) + shift_col) * scale
    out_ref[0, 2:3, :] = 0.2 * (0.1 + scores[4:5] * scores[4:5])


def correlate(offsets, left, right, above, below, west, east):
    lines, pixels = left.shape
    tiles, blocks, per = lines // TILE, lines // RIM, TILE // RIM
    rim = pl.BlockSpec((RIM, pixels), lambda t, o: (0, 0))
    side = pl.BlockSpec((1, RIM, PADDED), lambda t, o: (t, 0, 0))
    return pl.pallas_call(
        functools.partial(correlate_kernel, tiles),
        grid_spec=pltpu.PrefetchScalarGridSpec(
            num_scalar_prefetch=1,
            grid=(tiles,),
            in_specs=[
                pl.BlockSpec((TILE, pixels), lambda t, o: (t, 0)),
                pl.BlockSpec((TILE, pixels), lambda t, o: (t, 0)),
                pl.BlockSpec((RIM, pixels), lambda t, o: (jnp.maximum(t * per - 1, 0), 0)),
                pl.BlockSpec((RIM, pixels), lambda t, o: (jnp.minimum((t + 1) * per, blocks - 1), 0)),
                rim,
                rim,
                side,
                side,
            ],
            out_specs=pl.BlockSpec((1, 8, TILE), lambda t, o: (t, 0, 0)),
            scratch_shapes=[
                pltpu.VMEM((3, WINDOW, TILE), BF16),
                pltpu.VMEM((PADDED, LANES), F32),
                pltpu.VMEM((8, PADDED, LANES), F32),
                pltpu.VMEM((8, PADDED), F32),
                pltpu.VMEM((TILE // LANES, 3, LANES + 2 * RIM, LANES), F32),
                pltpu.VMEM((16, TILE), F32),
                pltpu.VMEM((16, TILE), F32),
                pltpu.VMEM((16, TILE), F32),
            ],
        ),
        out_shape=jax.ShapeDtypeStruct((tiles, 8, TILE), F32),
        name="correlate",
    )(offsets, left, right, right, right, above, below, west, east)


def bin_kernel(
    per_owner, obs_ref, owner_ref, source_ref, line_ref, out_ref, value_ref, spot_ref, hot_ref, part_ref, bins_ref
):
    tiles = obs_ref.shape[0]
    groups = owner_ref.shape[0] // 8
    match_rows = hot_ref.shape[1] // LANES
    bins = bins_ref.shape[1]
    sources = [source_ref[8 * g : 8 * g + 8, :] for g in range(groups)]
    high = [source // LANES for source in sources]
    low = [source % LANES for source in sources]
    fields = [[jnp.zeros((8, LANES), F32)] * groups for _ in range(3)]
    for t in range(tiles):
        for b in range(TILE // LANES):
            here = [h == t * (TILE // LANES) + b for h in high]
            for v in range(3):
                table = jnp.broadcast_to(
                    obs_ref[t, v : v + 1, LANES * b : LANES * (b + 1)], (8, LANES)
                )
                for g in range(groups):
                    taken = jnp.take_along_axis(table, low[g], axis=1, mode="promise_in_bounds")
                    fields[v][g] = jnp.where(here[g], taken, fields[v][g])
    for g in range(groups):
        rows = slice(8 * g, 8 * g + 8)
        line = line_ref[rows, :]
        far = ((line % SAMP).astype(F32) + 0.5) / SAMP
        near = 1.0 - far
        sample = owner_ref[rows, :] * per_owner + line // SAMP
        spot_ref[0, rows, :] = sample // LANES
        spot_ref[1, rows, :] = sample % LANES
        weight = fields[2][g]
        along, across = weight * fields[0][g], weight * fields[1][g]
        values = [
            weight * (near * near),
            weight * (far * far),
            weight * (far * near),
            along * near,
            along * far,
            across * near,
            across * far,
        ]
        for v in range(7):
            upper = values[v].astype(BF16).astype(F32)
            value_ref[v, 0, rows, :] = upper
            value_ref[v, 1, rows, :] = values[v] - upper
    for r in range(match_rows):
        hot = iota((LANES, LANES), 0) == spot_ref[1, r : r + 1, :]
        hot_ref[:, LANES * r : LANES * (r + 1)] = hot.astype(F32).astype(BF16)

    @pl.loop(0, 7)
    def _(v):
        for r in range(match_rows):
            here = iota((bins, LANES), 0) == spot_ref[0, r : r + 1, :]
            for p in range(2):
                part_ref[p, :, LANES * r : LANES * (r + 1)] = jnp.where(
                    here, value_ref[v, p, r : r + 1, :], 0.0
                ).astype(BF16)
        contract = (((1,), (1,)), ((), ()))
        bins_ref[v] = lax.dot_general(
            part_ref[0], hot_ref[...], contract, preferred_element_type=F32
        ) + lax.dot_general(part_ref[1], hot_ref[...], contract, preferred_element_type=F32)

    lane, row = iota((bins, LANES), 1), iota((bins, LANES), 0)
    for v in (1, 4, 6):
        turned = pltpu.roll(bins_ref[v], 1, 1)
        carried = jnp.where(row == 0, 0.0, pltpu.roll(turned, 1, 0))
        bins_ref[v - 1] = bins_ref[v - 1] + jnp.where(lane == 0, carried, turned)
    span = per_owner // LANES
    for d in range(bins // span):
        for i, v in enumerate((0, 2, 3, 5)):
            out_ref[d, span * i : span * (i + 1), :] = bins_ref[v, span * d : span * (d + 1), :]


def bin_matches(observations, owner, source, line, device_count, per_owner):
    count = source.shape[0]
    match_rows = count // LANES
    padded_rows = -(-match_rows // 8) * 8
    spare = padded_rows * LANES - count

    def lay(array, fill):
        return jnp.pad(array, (0, spare), constant_values=fill).reshape(padded_rows, LANES)

    bins = device_count * per_owner // LANES
    block = 4 * per_owner // LANES
    return pl.pallas_call(
        functools.partial(bin_kernel, per_owner),
        out_shape=jax.ShapeDtypeStruct((device_count, block, LANES), F32),
        scratch_shapes=[
            pltpu.VMEM((7, 2, padded_rows, LANES), F32),
            pltpu.VMEM((2, padded_rows, LANES), jnp.int32),
            pltpu.VMEM((LANES, match_rows * LANES), BF16),
            pltpu.VMEM((2, bins, match_rows * LANES), BF16),
            pltpu.VMEM((7, bins, LANES), F32),
        ],
        name="bin_matches",
    )(observations, lay(owner, 0), lay(source, 0), lay(line, 0))


def local(left_image, right_image, peak_offsets, match_owner, match_source, match_line):
    rows_dev = left_image.shape[0]
    seg_count = lax.axis_size("seg")
    col_count = lax.axis_size("col")
    device_count = seg_count * col_count
    samp_own = rows_dev // (SAMP * col_count)

    def forward(value, axis):
        size = lax.axis_size(axis)
        return lax.ppermute(value, axis, [(i, i + 1) for i in range(size - 1)])

    def backward(value, axis):
        size = lax.axis_size(axis)
        return lax.ppermute(value, axis, [(i + 1, i) for i in range(size - 1)])

    above = forward(right_image[rows_dev - RIM :], "seg")
    below = backward(right_image[:RIM], "seg")
    first_edge, last_edge = edges(right_image, above, below)
    west = forward(last_edge, "col")
    east = backward(first_edge, "col")
    observations = correlate(
        peak_offsets[:, :, 0], left_image, right_image, above, below, west, east
    )
    outgoing = bin_matches(
        observations, match_owner[:, 0], match_source, match_line, device_count, samp_own
    )
    received = lax.all_to_all(outgoing, ("seg", "col"), split_axis=0, concat_axis=0, tiled=True)
    by_column = jnp.sum(received.reshape(seg_count, col_count, 4, samp_own), axis=0)
    index_pairs = ((0, 0), (0, 1), (0, 2), (1, 1), (1, 2), (2, 2))
    diagonal, coupling, right_side = [0.0] * 6, [0.0] * 6, [0.0] * 3
    for column in range(col_count):
        spread = 2.0 * (column + 0.5) / col_count - 1.0
        along = (JACOBIAN_A * spread, 1.0, spread)
        across = (1.0, JACOBIAN_B * spread, JACOBIAN_C * spread)
        near, both, resid_row, resid_col = (by_column[column, i] for i in range(4))
        for i, (a, b) in enumerate(index_pairs):
            factor = along[a] * along[b] + across[a] * across[b]
            diagonal[i] = diagonal[i] + factor * near
            coupling[i] = coupling[i] + factor * both
        for a in range(3):
            right_side[a] = right_side[a] + along[a] * resid_row + across[a] * resid_col
    return (jnp.stack(diagonal), jnp.stack(coupling), jnp.stack(right_side))


def solution(mesh):
    return jax.shard_map(
        local,
        mesh=mesh,
        in_specs=(
            P("seg", "col"),
            P("seg", "col"),
            P(None, "seg", "col"),
            P(("seg", "col"), None),
            P(("seg", "col")),
            P(("seg", "col")),
        ),
        out_specs=(P(None, ("seg", "col")), P(None, ("seg", "col")), P(None, ("seg", "col"))),
        check_vma=False,
    )
```

time: 819 us -> 142 us (0.17); the launches traced: 809 us -> 141 us
  other arithmetic: 397 us -> 0.82 us
  local copies, waits for them, and re-layouts: 281 us -> 4.65 us
  Pallas kernels: 0 us -> 98.8 us
  loops' own time: 86.2 us -> 0 us
  starting transfers between devices: 29.9 us -> 8.9 us
  blocking collectives: 0 us -> 20.4 us
    scatter-add x5 -> x0, other arithmetic: 291 us -> none  [the longest x1 58.3 us: bin_terms(): diagonal.at[:, next_ids]]
    pallas_call x0 -> x3, Pallas kernels: none -> 98.8 us  [the longest x1 78.7 us: correlate(): pl.pallas_call(functools.partial(correlate_kernel, tiles), grid_spec=pltp...]
    another operation x1 -> x0, loops' own time: 86.2 us -> none  [local(): lax.map(one_tile, jnp.arange(rows_dev // TILE, dtype=jnp.int32))]
    slice x59 -> x1, local copies, waits for them, and re-layouts: 68.5 us -> 0.74 us  [local(): below = backward(right_image[:RIM], 'seg')]
    while x209 -> x0, local copies, waits for them, and re-layouts: 65.9 us -> none
    reduce_sum x113 -> x1, other arithmetic: 56.2 us -> 0.05 us  [local(): jnp.sum(received.reshape(seg_count, col_count, 4, samp_own), axis=0)]
    gather x1 -> x0, local copies, waits for them, and re-layouts: 35.5 us -> none  [local(): records = observations[match_source // TILE, :, match_source % TILE]]
    dynamic_slice x32 -> x0, local copies, waits for them, and re-layouts: 30 us -> none  [the longest x16 19.7 us: local(): lax.map(one_tile, jnp.arange(rows_dev // TILE, dtype=jnp.int32))]
  transfers between devices with their start and end apart: 8 -> 4, of which waited for: 2 -> 2; matrix products, arithmetic and copies ran while one was open for 13% -> 1% of each run, Pallas kernels for 0% -> 0%
where the time goes in v1:
time: 142 us; the launch traced here: 141 us
  Pallas kernels  98.8 us (70%)
  blocking collectives  20.4 us (14%)
  starting transfers between devices  8.9 us (6%)
  waiting for transfers between devices  7.18 us (5%)
  local copies, waits for them, and re-layouts  4.65 us (3%)
    pallas_call x1, Pallas kernels, correlate(): pl.pallas_call(functools.partial(correlate_kernel, tiles), grid_spec=pltp...  78.7 us
    all_to_all x1, blocking collectives, local(): lax.all_to_all(outgoing, ('seg', 'col'), split_axis=0, concat_axis=0, til...  20.4 us
    pallas_call x1, Pallas kernels, edges(): pl.pallas_call(functools.partial(edge_kernel, tiles), grid=(tiles,), in_s...  11.2 us
    pallas_call x1, Pallas kernels, bin_matches(): pl.pallas_call(functools.partial(bin_kernel, per_owner), out_shape=jax.Sh...  8.83 us
    ppermute x2, waiting for transfers between devices, backward(): return lax.ppermute(value, axis, [(i + 1, i) for i in range(size - 1)])  7.17 us
    ppermute x2, starting transfers between devices, forward(): return lax.ppermute(value, axis, [(i, i + 1) for i in range(size - 1)])  6.19 us
  transfers between devices with their start and end apart: 4, of which 2 were waited for; matrix products, arithmetic and copies ran while one was open for 1% of the time, Pallas kernels for 0%

profile of v1, /device:TPU:0, one launch (start us, length us, event | category | flops | bytes accessed | tf_op | source)
XLA Modules:
  0.0 141.5 jit_solution(2072907925223415141)
XLA Ops:
  0.6 0.7 fusion
  1.4 4.9 %collective-permute-start = (bf16[16,512]{1,0:T(8,128)(2,1)S(1)}, bf16[16,512]{1,0:T(8,128)(2,1)S(1)}, u32[]{:S(2)}, u32[]{:S(2)}) collective-permute-start(bf16[16,512]{1,0:T(8,128)(2,1)S(1)} %get-tuple-element.8), channel_id=1, source_target_pairs={{0,4},{4,8},{8,12},{12,16},{16,20},{20,24},{24,28},{1,5},{5,9},{9,... | collective-permute-start | bytes 49160 | tf_op jit(solution)/shard_map/ppermute | solution.py:376
  6.3 0.0 copy-start.6
  6.3 0.0 copy-start.4
  6.3 0.0 copy-start.5
  6.3 1.4 %collective-permute-start.1 = (bf16[16,512]{1,0:T(8,128)(2,1)S(1)}, bf16[16,512]{1,0:T(8,128)(2,1)S(1)}, u32[]{:S(2)}, u32[]{:S(2)}) collective-permute-start(bf16[16,512]{1,0:T(8,128)(2,1)S(1)} %get-tuple-element.7), channel_id=1, source_target_pairs={{4,0},{8,4},{12,8},{16,12},{20,16},{24,20},{28,24},{5,1},{9,5},{13... | collective-permute-start | bytes 49160 | tf_op jit(solution)/shard_map/ppermute | solution.py:380
  7.7 0.0 copy-start.2
  7.8 4.3 %collective-permute-done.1.refs_4_.refs_9_.below_ref = bf16[16,512]{1,0:T(8,128)(2,1)S(1)} collective-permute-done((bf16[16,512]{1,0:T(8,128)(2,1)S(1)}, bf16[16,512]{1,0:T(8,128)(2,1)S(1)}, u32[]{:S(2)}, u32[]{:S(2)}) %collective-permute-start.1) | collective-permute-done | bytes 16416 | tf_op jit(solution)/shard_map/ppermute | solution.py:380
  12.1 0.6 copy-done.3
  12.7 11.2 %edges.1 = (bf16[16,16,640]{2,1,0:T(8,128)(2,1)}, bf16[16,16,640]{2,1,0:T(8,128)(2,1)}) custom-call(bf16[8192,512]{1,0:T(8,128)(2,1)} %next_ref.1, bf16[8192,512]{1,0:T(8,128)(2,1)} %next_ref.1, bf16[8192,512]{1,0:T(8,128)(2,1)} %next_ref.1, bf16[16,512]{1,0:T(8,128)(2,1)} %copy-done.2, bf16[16,512]{1,0:T(8,128)(2,1)} %copy-done.3, ...), custom_call_target="tpu_custom_call" | custom-call | tf_op jit(solution)/shard_map/edges/pallas_call | solution.py:73
  23.9 1.3 collective-permute-start.2
  25.2 1.3 collective-permute-start.3
  26.6 0.6 pad_bitcast_fusion.2.owner_ref
  27.2 0.6 pad_bitcast_fusion
  27.8 2.9 %collective-permute-done.3.east_ref = bf16[16,16,640]{2,1,0:T(8,128)(2,1)S(1)} collective-permute-done((bf16[16,16,640]{2,1,0:T(8,128)(2,1)}, bf16[16,16,640]{2,1,0:T(8,128)(2,1)S(1)}, u32[]{:S(2)}, u32[]{:S(2)}) %collective-permute-start.3) | collective-permute-done | bytes 327712 | tf_op jit(solution)/shard_map/ppermute | solution.py:380
  30.7 0.7 copy-done.1
  31.4 78.7 %correlate.1.obs_ref = f32[16,8,512]{2,1,0:T(8,128)} custom-call(s32[2,16]{1,0:T(2,128)} %bitcast.95, bf16[8192,512]{1,0:T(8,128)(2,1)} %left_ref.1, bf16[8192,512]{1,0:T(8,128)(2,1)} %next_ref.1, bf16[8192,512]{1,0:T(8,128)(2,1)} %next_ref.1, bf16[8192,512]{1,0:T(8,128)(2,1)} %next_ref.1, bf16[16,512]{1,0:T(8,128)(2,1)} %copy-done.2, ...), custom_call_target="tpu_custom_call" | custom-call | tf_op jit(solution)/shard_map/correlate/pallas_call | solution.py:238
  110.1 8.8 %bin_matches.1 = f32[32,16,128]{2,1,0:T(8,128)} custom-call(f32[16,8,512]{2,1,0:T(8,128)} %correlate.1.obs_ref, s32[32,128]{1,0:T(8,128)} %pad_bitcast_fusion.2.owner_ref, s32[32,128]{1,0:T(8,128)} %get-tuple-element.24.source_ref, s32[32,128]{1,0:T(8,128)} %get-tuple-element.23.line_ref), custom_call_target="tpu_custom_call" | custom-call | tf_op jit(solution)/shard_map/bin_matches/pallas_call | solution.py:353
  118.9 20.4 %all_to_all.5 = f32[32,16,128]{2,1,0:T(8,128)S(1)} all-to-all(f32[32,16,128]{2,1,0:T(8,128)} %bin_matches.1), channel_id=1, replica_groups=mesh['seg'=8,'col'=4] {'seg','col'}, dimensions={0} | all-to-all | bytes 524288 | tf_op jit(solution)/shard_map/all_to_all | solution.py:393
  139.3 0.1 reshape.1020
  139.4 0.1 reduce_sum.9
  139.6 0.6 pad_maximum_fusion
  140.2 0.6 stack.7
  140.9 0.6 stack.6
  (16 shorter events, 0.2 us)
Async XLA Ops:
  1.4 6.4 %collective-permute-start = (bf16[16,512]{1,0:T(8,128)(2,1)S(1)}, bf16[16,512]{1,0:T(8,128)(2,1)S(1)}, u32[]{:S(2)}, u32[]{:S(2)}) collective-permute-start(bf16[16,512]{1,0:T(8,128)(2,1)S(1)} %get-tuple-element.8), channel_id=1, source_target_pairs={{0,4},{4,8},{8,12},{12,16},{16,20},{20,24},{24,28},{1,5},{5,9},{9,... | collective-permute-start | bytes 49160 | tf_op jit(solution)/shard_map/ppermute | solution.py:376
  6.3 20.3 %copy-start.6 = (s32[3584,1]{0,1:T(1,128)S(1)}, s32[3584,1]{0,1:T(1,128)}, u32[]{:S(2)}) copy-start(s32[3584,1]{0,1:T(1,128)} %param.9) | copy-start | bytes 43012
  6.3 20.9 %copy-start.4 = (s32[3584]{0:T(1024)S(1)}, s32[3584]{0:T(1024)}, u32[]{:S(2)}) copy-start(s32[3584]{0:T(1024)} %param.11) | copy-start | bytes 43012
  6.3 20.9 %copy-start.5 = (s32[3584]{0:T(1024)S(1)}, s32[3584]{0:T(1024)}, u32[]{:S(2)}) copy-start(s32[3584]{0:T(1024)} %param.10) | copy-start | bytes 43012
  6.3 5.8 %collective-permute-start.1 = (bf16[16,512]{1,0:T(8,128)(2,1)S(1)}, bf16[16,512]{1,0:T(8,128)(2,1)S(1)}, u32[]{:S(2)}, u32[]{:S(2)}) collective-permute-start(bf16[16,512]{1,0:T(8,128)(2,1)S(1)} %get-tuple-element.7), channel_id=1, source_target_pairs={{4,0},{8,4},{12,8},{16,12},{20,16},{24,20},{28,24},{5,1},{9,5},{13... | collective-permute-start | bytes 49160 | tf_op jit(solution)/shard_map/ppermute | solution.py:380
  7.7 4.3 %copy-start.2 = (bf16[16,512]{1,0:T(8,128)(2,1)}, bf16[16,512]{1,0:T(8,128)(2,1)S(1)}, u32[]{:S(2)}) copy-start(bf16[16,512]{1,0:T(8,128)(2,1)S(1)} %collective-permute-done.refs_3_.refs_8_.above_ref) | copy-start | bytes 49156
  12.1 0.6 copy-start.3
  23.9 3.9 %collective-permute-start.2 = (bf16[16,16,640]{2,1,0:T(8,128)(2,1)}, bf16[16,16,640]{2,1,0:T(8,128)(2,1)S(1)}, u32[]{:S(2)}, u32[]{:S(2)}) collective-permute-start(bf16[16,16,640]{2,1,0:T(8,128)(2,1)} %get-tuple-element.5), channel_id=1, source_target_pairs={{0,1},{1,2},{2,3},{4,5},{5,6},{6,7},{8,9},{9,10},{10,11},{12,13},{... | collective-permute-start | bytes 983048 | tf_op jit(solution)/shard_map/ppermute | solution.py:376
  25.2 5.4 %collective-permute-start.3 = (bf16[16,16,640]{2,1,0:T(8,128)(2,1)}, bf16[16,16,640]{2,1,0:T(8,128)(2,1)S(1)}, u32[]{:S(2)}, u32[]{:S(2)}) collective-permute-start(bf16[16,16,640]{2,1,0:T(8,128)(2,1)} %get-tuple-element.6), channel_id=1, source_target_pairs={{1,0},{2,1},{3,2},{5,4},{6,5},{7,6},{9,8},{10,9},{11,10},{13,12},{... | collective-permute-start | bytes 983048 | tf_op jit(solution)/shard_map/ppermute | solution.py:380
  27.8 2.9 %copy-start = (bf16[16,16,640]{2,1,0:T(8,128)(2,1)}, bf16[16,16,640]{2,1,0:T(8,128)(2,1)S(1)}, u32[]{:S(2)}) copy-start(bf16[16,16,640]{2,1,0:T(8,128)(2,1)S(1)} %collective-permute-done.2.west_ref) | copy-start | bytes 983044
  30.7 0.7 copy-start.1

commit v2 on v1

--- a/solution.py
+++ b/solution.py
@@ -35,31 +35,39 @@
     return before, after
 
 
-def edge_kernel(tiles, *refs):
+def edge_kernel(steps, per_step, *refs):
     sides, outs = (refs[:5], refs[5:10]), refs[10:]
-    tile = pl.program_id(0)
+    step = pl.program_id(0)
+    contract = (((1,), (1,)), ((), ()))
     for side in range(2):
         main_ref, prev_ref, next_ref, above_ref, below_ref = sides[side]
-        before, after = rim_rows(tile, tiles, prev_ref, next_ref, above_ref, below_ref)
-        wrap = jnp.concatenate(
-            [after, jnp.zeros((LANES - 2 * RIM, LANES), F32), before], axis=0
-        ).astype(BF16)
+        before, after = rim_rows(step, steps, prev_ref, next_ref, above_ref, below_ref)
         first = 0 if side == 0 else LANES - RIM
         pick = (iota((RIM, LANES), 1) == iota((RIM, LANES), 0) + first).astype(F32).astype(BF16)
-        contract = (((1,), (1,)), ((), ()))
-        main = lax.dot_general(pick, main_ref[...], contract, preferred_element_type=F32)
-        rest = lax.dot_general(pick, wrap, contract, preferred_element_type=F32)
-        outs[side][0, :, :TILE] = main.astype(BF16)
-        outs[side][0, :, TILE:] = rest.astype(BF16)
+        zeros = jnp.zeros((LANES - 2 * RIM, LANES), F32)
+        for tile in range(per_step):
+            start = tile * TILE
+            head = before if tile == 0 else main_ref[start - RIM : start, :].astype(F32)
+            stop = start + TILE
+            tail = after if tile == per_step - 1 else main_ref[stop : stop + RIM, :].astype(F32)
+            wrap = jnp.concatenate([tail, zeros, head], axis=0).astype(BF16)
+            main = lax.dot_general(
+                pick, main_ref[start:stop, :], contract, preferred_element_type=F32
+            )
+            rest = lax.dot_general(pick, wrap, contract, preferred_element_type=F32)
+            outs[side][tile, :, :TILE] = main.astype(BF16)
+            outs[side][tile, :, TILE:] = rest.astype(BF16)
 
 
 def edges(right, above, below):
     lines, pixels = right.shape
-    tiles, blocks, per = lines // TILE, lines // RIM, TILE // RIM
+    tiles, blocks = lines // TILE, lines // RIM
+    per_step = 4 if tiles % 4 == 0 else 1
+    steps, per = tiles // per_step, per_step * TILE // RIM
     specs, operands = [], []
     for block in (0, pixels // LANES - 1):
         specs += [
-            pl.BlockSpec((TILE, LANES), lambda t, block=block: (t, block)),
+            pl.BlockSpec((per_step * TILE, LANES), lambda t, block=block: (t, block)),
             pl.BlockSpec((RIM, LANES), lambda t, block=block: (jnp.maximum(t * per - 1, 0), block)),
             pl.BlockSpec(
                 (RIM, LANES),
@@ -71,10 +79,10 @@
         operands += [right, right, right, above, below]
     out = jax.ShapeDtypeStruct((tiles, RIM, PADDED), BF16)
     return pl.pallas_call(
-        functools.partial(edge_kernel, tiles),
-        grid=(tiles,),
+        functools.partial(edge_kernel, steps, per_step),
+        grid=(steps,),
         in_specs=specs,
-        out_specs=[pl.BlockSpec((1, RIM, PADDED), lambda t: (t, 0, 0))] * 2,
+        out_specs=[pl.BlockSpec((per_step, RIM, PADDED), lambda t: (t, 0, 0))] * 2,
         out_shape=[out, out],
         name="edges",
     )(*operands)
@@ -104,7 +112,9 @@
     out_ref,
     shifted_ref,
     halo_ref,
-    stat_ref,
+    window_ref,
+    window_square_ref,
+    left_square_ref,
     flat_ref,
     gram_ref,
     dots_ref,
@@ -127,11 +137,23 @@
         contract,
         preferred_element_type=F32,
     )
-    halo_ref[...] = east + west
+    halo_ref[...] = (east + west).astype(BF16)
+
+    def split_squares(values, square_ref, target, place):
+        rows, width = values.shape
+        square = values.astype(F32) * values.astype(F32)
+        upper = square.astype(BF16)
+        square_ref[0, pl.ds(target, rows), place : place + width] = upper
+        square_ref[1, pl.ds(target, rows), place : place + width] = (
+            square - upper.astype(F32)
+        ).astype(BF16)
 
     def process(values, halo, target):
         rows = values.shape[0]
         parts = [values[:, LANES * b : LANES * (b + 1)] for b in range(blocks)] + [halo]
+        for b in range(blocks + 1):
+            window_ref[pl.ds(target, rows), LANES * b : LANES * (b + 1)] = parts[b]
+            split_squares(parts[b], window_square_ref, target, LANES * b)
         lane = iota((rows, LANES), 1)
         for s in range(3):
             step = offset_col + (s - 1)
@@ -139,58 +161,56 @@
             turned = [pltpu.roll(part, turn, 1) for part in parts]
             source = lane + step
             low, high = source < 0, source >= LANES
-            total = squares = None
             for b in range(blocks):
-                value = jnp.where(
+                shifted_ref[s, pl.ds(target, rows), LANES * b : LANES * (b + 1)] = jnp.where(
                     low, turned[b - 1], jnp.where(high, turned[b + 1], turned[b])
                 )
-                total = value if b == 0 else total + value
-                squares = value * value if b == 0 else squares + value * value
-                shifted_ref[s, pl.ds(target, rows), LANES * b : LANES * (b + 1)] = value.astype(BF16)
-            stat_ref[s, pl.ds(target, rows), :] = jnp.broadcast_to(
-                jnp.sum(total, axis=1, keepdims=True), (rows, LANES)
-            )
-            stat_ref[3 + s, pl.ds(target, rows), :] = jnp.broadcast_to(
-                jnp.sum(squares, axis=1, keepdims=True), (rows, LANES)
-            )
 
     before, after = rim_rows(tile, tiles, prev_ref, next_ref, above_ref, below_ref)
-    process(before, halo_ref[PADDED - RIM :, :], 0)
-    process(after, halo_ref[TILE : TILE + RIM, :], RIM + TILE)
-    chunk = 32
+    process(before.astype(BF16), halo_ref[PADDED - RIM :, :], 0)
+    process(after.astype(BF16), halo_ref[TILE : TILE + RIM, :], RIM + TILE)
+    chunk = 64
 
     @pl.loop(0, TILE // chunk)
     def _(index):
         start = pl.multiple_of(index * chunk, chunk)
         process(
-            main_ref[pl.ds(start, chunk), :].astype(F32),
+            main_ref[pl.ds(start, chunk), :],
             halo_ref[pl.ds(start, chunk), :],
             pl.multiple_of(start + RIM, RIM),
         )
-        left = left_ref[pl.ds(start, chunk), :].astype(F32)
-        parts = [left[:, LANES * b : LANES * (b + 1)] for b in range(blocks)]
-        total = parts[0] + parts[1] + parts[2] + parts[3]
-        squares = sum(part * part for part in parts[1:]) + parts[0] * parts[0]
-        stat_ref[6, pl.ds(start, chunk), :] = jnp.broadcast_to(
-            jnp.sum(total, axis=1, keepdims=True), (chunk, LANES)
-        )
-        stat_ref[7, pl.ds(start, chunk), :] = jnp.broadcast_to(
-            jnp.sum(squares, axis=1, keepdims=True), (chunk, LANES)
-        )
-
-    for k in range(8):
-        for b in range(5 if k < 6 else 4):
-            flat_ref[k : k + 1, LANES * b : LANES * (b + 1)] = pick_lines(
-                lambda i: stat_ref[k, LANES * b + 8 * i : LANES * b + 8 * i + 8, :],
-                16 if b < 4 else 4,
-            )
+        split_squares(left_ref[pl.ds(start, chunk), :], left_square_ref, start, 0)
+
+    def mask_rows(width, first, last):
+        row, pixel = iota((16, width), 0), iota((16, width), 1)
+        place = pixel - (offset_col - 1 + row % 3)
+        place = jnp.where(place < 0, place + PADDED, place)
+        place = jnp.where(place >= PADDED, place - PADDED, place)
+        inside = (place < TILE) & (row >= first) & (row < last)
+        return inside.astype(F32).astype(BF16)
+
+    def line_sums(mask, lines):
+        return lax.dot_general(mask, lines, (((1,), (1,)), ((), ())), preferred_element_type=F32)
+
+    sum_mask, square_mask = mask_rows(PADDED, 0, 3), mask_rows(PADDED, 3, 6)
+    flat_ref[...] = (
+        line_sums(sum_mask, window_ref[...])
+        + line_sums(square_mask, window_square_ref[0])
+        + line_sums(square_mask, window_square_ref[1])
+    )
+    row = iota((16, TILE), 0)
+    left_sums = (
+        line_sums((row == 0).astype(F32).astype(BF16), left_ref[...])
+        + line_sums((row == 1).astype(F32).astype(BF16), left_square_ref[0])
+        + line_sums((row == 1).astype(F32).astype(BF16), left_square_ref[1])
+    )
 
     lane = iota((8, LANES), 1)
     for r in range(3):
         start = offset_row + (RANGE + r)
         turn = lax.rem(LANES - start, LANES)
         turned = [
-            pltpu.roll(flat_ref[:, LANES * b : LANES * (b + 1)], turn, 1) for b in range(blocks + 1)
+            pltpu.roll(flat_ref[0:8, LANES * b : LANES * (b + 1)], turn, 1) for b in range(blocks + 1)
         ]
         for b in range(blocks):
             value = jnp.where(lane < LANES - start, turned[b], turned[b + 1])
@@ -213,8 +233,8 @@
                 )
 
     count = float(TILE)
-    left_sum = flat_ref[6:7, :TILE]
-    left_var = flat_ref[7:8, :TILE] - left_sum * left_sum / count + count * EPSILON
+    left_sum = left_sums[0:1]
+    left_var = left_sums[1:2] - left_sum * left_sum / count + count * EPSILON
     right_sum = sums_ref[0:9, :]
     right_var = squares_ref[0:9, :] - right_sum * right_sum / count + count * EPSILON
     covariance = dots_ref[0:9, :] - left_sum * right_sum / count
@@ -253,9 +273,11 @@
             out_specs=pl.BlockSpec((1, 8, TILE), lambda t, o: (t, 0, 0)),
             scratch_shapes=[
                 pltpu.VMEM((3, WINDOW, TILE), BF16),
-                pltpu.VMEM((PADDED, LANES), F32),
-                pltpu.VMEM((8, PADDED, LANES), F32),
-                pltpu.VMEM((8, PADDED), F32),
+                pltpu.VMEM((PADDED, LANES), BF16),
+                pltpu.VMEM((PADDED, PADDED), BF16),
+                pltpu.VMEM((2, PADDED, PADDED), BF16),
+                pltpu.VMEM((2, TILE, TILE), BF16),
+                pltpu.VMEM((16, PADDED), F32),
                 pltpu.VMEM((TILE // LANES, 3, LANES + 2 * RIM, LANES), F32),
                 pltpu.VMEM((16, TILE), F32),
                 pltpu.VMEM((16, TILE), F32),

time: 142 us -> 120 us (0.85)
  Pallas kernels: 98.8 us -> 77.3 us
    pallas_call x1, Pallas kernels: 78.7 us -> 63.5 us  [correlate(): pl.pallas_call(functools.partial(correlate_kernel, tiles), grid_spec=pltp...]
    pallas_call x1, Pallas kernels: 11.2 us -> 4.98 us  [edges(): pl.pallas_call(functools.partial(edge_kernel, steps, per_step), grid=(ste...]
where the time goes in v2:
time: 120 us
  Pallas kernels  77.3 us (64%)
  blocking collectives  20.3 us (17%)
  starting transfers between devices  8.9 us (7%)
  waiting for transfers between devices  7.18 us (6%)
  local copies, waits for them, and re-layouts  4.65 us (4%)
    pallas_call x1, Pallas kernels, correlate(): pl.pallas_call(functools.partial(correlate_kernel, tiles), grid_spec=pltp...  63.5 us
    all_to_all x1, blocking collectives, local(): lax.all_to_all(outgoing, ('seg', 'col'), split_axis=0, concat_axis=0, til...  20.3 us
    pallas_call x1, Pallas kernels, bin_matches(): pl.pallas_call(functools.partial(bin_kernel, per_owner), out_shape=jax.Sh...  8.82 us
    ppermute x2, waiting for transfers between devices, backward(): return lax.ppermute(value, axis, [(i + 1, i) for i in range(size - 1)])  7.17 us
    ppermute x2, starting transfers between devices, forward(): return lax.ppermute(value, axis, [(i, i + 1) for i in range(size - 1)])  6.19 us
    pallas_call x1, Pallas kernels, edges(): pl.pallas_call(functools.partial(edge_kernel, steps, per_step), grid=(ste...  4.98 us
    ppermute x2, starting transfers between devices, backward(): return lax.ppermute(value, axis, [(i + 1, i) for i in range(size - 1)])  2.72 us
  transfers between devices with their start and end apart: 4, of which 2 were waited for; matrix products, arithmetic and copies ran while one was open for 1% of the time, Pallas kernels for 0%

profile of v2, /device:TPU:0, one launch (start us, length us, event | category | flops | bytes accessed | tf_op | source)
XLA Modules:
  0.0 119.9 jit_solution(5880457541669948807)
XLA Ops:
  0.6 0.7 fusion
  1.4 4.9 %collective-permute-start = (bf16[16,512]{1,0:T(8,128)(2,1)S(1)}, bf16[16,512]{1,0:T(8,128)(2,1)S(1)}, u32[]{:S(2)}, u32[]{:S(2)}) collective-permute-start(bf16[16,512]{1,0:T(8,128)(2,1)S(1)} %get-tuple-element.8), channel_id=1, source_target_pairs={{0,4},{4,8},{8,12},{12,16},{16,20},{20,24},{24,28},{1,5},{5,9},{9,... | collective-permute-start | bytes 49160 | tf_op jit(solution)/shard_map/ppermute | solution.py:398
  6.3 0.0 copy-start.6
  6.3 0.0 copy-start.4
  6.3 0.0 copy-start.5
  6.3 1.4 %collective-permute-start.1 = (bf16[16,512]{1,0:T(8,128)(2,1)S(1)}, bf16[16,512]{1,0:T(8,128)(2,1)S(1)}, u32[]{:S(2)}, u32[]{:S(2)}) collective-permute-start(bf16[16,512]{1,0:T(8,128)(2,1)S(1)} %get-tuple-element.7), channel_id=1, source_target_pairs={{4,0},{8,4},{12,8},{16,12},{20,16},{24,20},{28,24},{5,1},{9,5},{13... | collective-permute-start | bytes 49160 | tf_op jit(solution)/shard_map/ppermute | solution.py:402
  7.7 0.0 copy-start.2
  7.8 4.3 %collective-permute-done.1.refs_4_.refs_9_.below_ref = bf16[16,512]{1,0:T(8,128)(2,1)S(1)} collective-permute-done((bf16[16,512]{1,0:T(8,128)(2,1)S(1)}, bf16[16,512]{1,0:T(8,128)(2,1)S(1)}, u32[]{:S(2)}, u32[]{:S(2)}) %collective-permute-start.1) | collective-permute-done | bytes 16416 | tf_op jit(solution)/shard_map/ppermute | solution.py:402
  12.1 0.6 copy-done.3
  12.7 5.0 %edges.1 = (bf16[16,16,640]{2,1,0:T(8,128)(2,1)}, bf16[16,16,640]{2,1,0:T(8,128)(2,1)}) custom-call(bf16[8192,512]{1,0:T(8,128)(2,1)} %next_ref.1, bf16[8192,512]{1,0:T(8,128)(2,1)} %next_ref.1, bf16[8192,512]{1,0:T(8,128)(2,1)} %next_ref.1, bf16[16,512]{1,0:T(8,128)(2,1)} %copy-done.2, bf16[16,512]{1,0:T(8,128)(2,1)} %copy-done.3, ...), custom_call_target="tpu_custom_call" | custom-call | tf_op jit(solution)/shard_map/edges/pallas_call | solution.py:81
  17.7 1.3 %collective-permute-start.2 = (bf16[16,16,640]{2,1,0:T(8,128)(2,1)}, bf16[16,16,640]{2,1,0:T(8,128)(2,1)S(1)}, u32[]{:S(2)}, u32[]{:S(2)}) collective-permute-start(bf16[16,16,640]{2,1,0:T(8,128)(2,1)} %get-tuple-element.5), channel_id=1, source_target_pairs={{0,1},{1,2},{2,3},{4,5},{5,6},{6,7},{8,9},{9,10},{10,11},{12,13},{... | collective-permute-start | bytes 983048 | tf_op jit(solution)/shard_map/ppermute | solution.py:398
  19.0 1.3 %collective-permute-start.3 = (bf16[16,16,640]{2,1,0:T(8,128)(2,1)}, bf16[16,16,640]{2,1,0:T(8,128)(2,1)S(1)}, u32[]{:S(2)}, u32[]{:S(2)}) collective-permute-start(bf16[16,16,640]{2,1,0:T(8,128)(2,1)} %get-tuple-element.6), channel_id=1, source_target_pairs={{1,0},{2,1},{3,2},{5,4},{6,5},{7,6},{9,8},{10,9},{11,10},{13,12},{... | collective-permute-start | bytes 983048 | tf_op jit(solution)/shard_map/ppermute | solution.py:402
  20.3 0.6 pad_bitcast_fusion.2.owner_ref
  20.9 0.6 pad_bitcast_fusion
  21.5 2.9 %collective-permute-done.3.east_ref = bf16[16,16,640]{2,1,0:T(8,128)(2,1)S(1)} collective-permute-done((bf16[16,16,640]{2,1,0:T(8,128)(2,1)}, bf16[16,16,640]{2,1,0:T(8,128)(2,1)S(1)}, u32[]{:S(2)}, u32[]{:S(2)}) %collective-permute-start.3) | collective-permute-done | bytes 327712 | tf_op jit(solution)/shard_map/ppermute | solution.py:402
  24.4 0.7 copy-done.1
  25.1 63.5 %correlate.1.obs_ref = f32[16,8,512]{2,1,0:T(8,128)} custom-call(s32[2,16]{1,0:T(2,128)} %bitcast.95, bf16[8192,512]{1,0:T(8,128)(2,1)} %left_ref.1, bf16[8192,512]{1,0:T(8,128)(2,1)} %next_ref.1, bf16[8192,512]{1,0:T(8,128)(2,1)} %next_ref.1, bf16[8192,512]{1,0:T(8,128)(2,1)} %next_ref.1, bf16[16,512]{1,0:T(8,128)(2,1)} %copy-done.2, ...), custom_call_target="tpu_custom_call" | custom-call | tf_op jit(solution)/shard_map/correlate/pallas_call | solution.py:258
  88.6 8.8 %bin_matches.1 = f32[32,16,128]{2,1,0:T(8,128)} custom-call(f32[16,8,512]{2,1,0:T(8,128)} %correlate.1.obs_ref, s32[32,128]{1,0:T(8,128)} %pad_bitcast_fusion.2.owner_ref, s32[32,128]{1,0:T(8,128)} %get-tuple-element.24.source_ref, s32[32,128]{1,0:T(8,128)} %get-tuple-element.23.line_ref), custom_call_target="tpu_custom_call" | custom-call | tf_op jit(solution)/shard_map/bin_matches/pallas_call | solution.py:375
  97.4 20.3 %all_to_all.5 = f32[32,16,128]{2,1,0:T(8,128)S(1)} all-to-all(f32[32,16,128]{2,1,0:T(8,128)} %bin_matches.1), channel_id=1, replica_groups=mesh['seg'=8,'col'=4] {'seg','col'}, dimensions={0} | all-to-all | bytes 524288 | tf_op jit(solution)/shard_map/all_to_all | solution.py:415
  117.7 0.1 reshape.1020
  117.8 0.1 reduce_sum.9
  118.1 0.6 pad_maximum_fusion
  118.7 0.6 stack.7
  119.3 0.6 stack.6
  (16 shorter events, 0.2 us)
Async XLA Ops:
  1.4 6.4 %collective-permute-start = (bf16[16,512]{1,0:T(8,128)(2,1)S(1)}, bf16[16,512]{1,0:T(8,128)(2,1)S(1)}, u32[]{:S(2)}, u32[]{:S(2)}) collective-permute-start(bf16[16,512]{1,0:T(8,128)(2,1)S(1)} %get-tuple-element.8), channel_id=1, source_target_pairs={{0,4},{4,8},{8,12},{12,16},{16,20},{20,24},{24,28},{1,5},{5,9},{9,... | collective-permute-start | bytes 49160 | tf_op jit(solution)/shard_map/ppermute | solution.py:398
  6.3 14.0 %copy-start.6 = (s32[3584,1]{0,1:T(1,128)S(1)}, s32[3584,1]{0,1:T(1,128)}, u32[]{:S(2)}) copy-start(s32[3584,1]{0,1:T(1,128)} %param.9) | copy-start | bytes 43012
  6.3 14.6 %copy-start.4 = (s32[3584]{0:T(1024)S(1)}, s32[3584]{0:T(1024)}, u32[]{:S(2)}) copy-start(s32[3584]{0:T(1024)} %param.11) | copy-start | bytes 43012
  6.3 14.6 %copy-start.5 = (s32[3584]{0:T(1024)S(1)}, s32[3584]{0:T(1024)}, u32[]{:S(2)}) copy-start(s32[3584]{0:T(1024)} %param.10) | copy-start | bytes 43012
  6.3 5.8 %collective-permute-start.1 = (bf16[16,512]{1,0:T(8,128)(2,1)S(1)}, bf16[16,512]{1,0:T(8,128)(2,1)S(1)}, u32[]{:S(2)}, u32[]{:S(2)}) collective-permute-start(bf16[16,512]{1,0:T(8,128)(2,1)S(1)} %get-tuple-element.7), channel_id=1, source_target_pairs={{4,0},{8,4},{12,8},{16,12},{20,16},{24,20},{28,24},{5,1},{9,5},{13... | collective-permute-start | bytes 49160 | tf_op jit(solution)/shard_map/ppermute | solution.py:402
  7.7 4.3 %copy-start.2 = (bf16[16,512]{1,0:T(8,128)(2,1)}, bf16[16,512]{1,0:T(8,128)(2,1)S(1)}, u32[]{:S(2)}) copy-start(bf16[16,512]{1,0:T(8,128)(2,1)S(1)} %collective-permute-done.refs_3_.refs_8_.above_ref) | copy-start | bytes 49156
  12.1 0.6 copy-start.3
  17.7 3.9 %collective-permute-start.2 = (bf16[16,16,640]{2,1,0:T(8,128)(2,1)}, bf16[16,16,640]{2,1,0:T(8,128)(2,1)S(1)}, u32[]{:S(2)}, u32[]{:S(2)}) collective-permute-start(bf16[16,16,640]{2,1,0:T(8,128)(2,1)} %get-tuple-element.5), channel_id=1, source_target_pairs={{0,1},{1,2},{2,3},{4,5},{5,6},{6,7},{8,9},{9,10},{10,11},{12,13},{... | collective-permute-start | bytes 983048 | tf_op jit(solution)/shard_map/ppermute | solution.py:398
  19.0 5.4 %collective-permute-start.3 = (bf16[16,16,640]{2,1,0:T(8,128)(2,1)}, bf16[16,16,640]{2,1,0:T(8,128)(2,1)S(1)}, u32[]{:S(2)}, u32[]{:S(2)}) collective-permute-start(bf16[16,16,640]{2,1,0:T(8,128)(2,1)} %get-tuple-element.6), channel_id=1, source_target_pairs={{1,0},{2,1},{3,2},{5,4},{6,5},{7,6},{9,8},{10,9},{11,10},{13,12},{... | collective-permute-start | bytes 983048 | tf_op jit(solution)/shard_map/ppermute | solution.py:402
  21.5 2.9 %copy-start = (bf16[16,16,640]{2,1,0:T(8,128)(2,1)}, bf16[16,16,640]{2,1,0:T(8,128)(2,1)S(1)}, u32[]{:S(2)}) copy-start(bf16[16,16,640]{2,1,0:T(8,128)(2,1)S(1)} %collective-permute-done.2.west_ref) | copy-start | bytes 983044
  24.4 0.7 copy-start.1
